TPU v7x, 32 devices: a whole 2x2x4 slice. The times are simulated.
32 devices in a mesh: we: 4 (over y, x), sn: 8 (over z, core).
Axes of the slice: x: 2, y: 2, z: 4, core: 2. Of those that a mesh axis runs over, the one named last changes fastest.
Arguments:
- velocity: float32 [3, 16, 96, 128], P(None, 'we', 'sn'), may hold values from -6 to 6
- stress: float32 [6, 16, 96, 128], P(None, 'we', 'sn'), may hold values from -6 to 6
- memory: float32 [6, 16, 96, 128], P(None, 'we', 'sn'), may hold values from -3 to 3
- material_code: int32 [16, 96, 128], P('we', 'sn'), may hold values from 0 to 15
- block_scale: float32 [4, 24, 4], P('we', 'sn'), may hold values from 0.5 to 2
- material_table: float32 [6, 16], replicated, may hold values from 0.2 to 3, as said below
- source_cell: int32 [4, 8, 4], P('we', 'sn'), may hold values from 0 to 6143, as said below
- source_amp: float32 [4, 8, 4, 4], P('we', 'sn'), may hold values from -24 to 24
Outputs:
- velocity_out: float32 [3, 16, 96, 128], P(None, 'we', 'sn')
- stress_out: float32 [6, 16, 96, 128], P(None, 'we', 'sn')
- memory_out: float32 [6, 16, 96, 128], P(None, 'we', 'sn')
Inputs may be any that keep to these rules, and one draw needn't show every extreme that they name: Rows of material_table lie in: buoyancy 0.6 to 1.4, first Lame parameter 0.5 to 2, shear modulus 0.3 to 1.5, decay 0.5 to 0.98, weight 0.2 to 0.8, cohesion 0.3 to 3. `source_cell`: each entry is c = x 12 * 128 + y * 128 + z for a cell (x, y, z) of the device's own block; cells may repeat.
All inputs are finite; a program needn't handle non-finite values.
Results may differ from a plain program's by a relative error of at most 0.0001.
Values sent between devices are 32-bit elements; how exact they have to be, the bound alone decides.
No kernel may reach another device: no remote copies, remote signals or barrier semaphores. Data moves between devices by JAX's collectives and lax.ppermute only.
A program may use at most 64 MiB of HBM per device.

v0:
```python
import functools

import jax
import jax.numpy as jnp
from jax import lax
from jax.experimental import pallas as pl
from jax.experimental.pallas import tpu as pltpu
from jax.sharding import PartitionSpec as P


BLK = 4
BLKZ = 32
LANES = 128
SUB = 8

inner_coef = 9.0 / 8.0
outer_coef = 1.0 / 24.0
ratio = outer_coef / inner_coef
time_step = 0.08
friction = 0.4
half_step = 0.5 * time_step
largest = 3.0e38

VEL, STR, MEM, COD = 0, 3, 9, 15
FIELDS = 16
SPLIT = 8
WHOLE, FIRST, SECOND = 0, 1, 2
HELD = (range(FIELDS), range(SPLIT), range(SPLIT, FIELDS))
NORMAL = (0, 4, 5)
UNROLL = (16, 14)


def round_up(value, step):
    return -(-value // step) * step


def pack_kernel(vel, stress, mem, code, scale, cell, amp, kinds, out, table, sem, *, field):
    copies = []
    for i, (at, part) in enumerate(((VEL, vel), (STR, stress), (MEM, mem))):
        to = out.at[pl.ds(at * field, part.shape[0]), :]
        copies.append(pltpu.make_async_copy(part, to, sem.at[i]))
        copies[-1].start()
    out[COD * field : (COD + 1) * field, :] = (code[...] + 1).astype(jnp.float32)
    lane = lax.broadcasted_iota(jnp.int32, (1, LANES), 1)
    here = FIELDS * field
    for i in range(scale.shape[1]):
        for j in range(scale.shape[0]):
            row = jnp.zeros((1, LANES), jnp.float32)
            for k in range(scale.shape[2]):
                row = jnp.where(lane // BLKZ == k, scale[j, i, k], row)
            out[here : here + 1, :] = row
            here += 1
    size = out.shape[0]
    if here < size - 1:
        out[here : size - 1, :] = jnp.zeros((size - 1 - here, LANES), jnp.float32)
    count, steps = amp.shape[2], amp.shape[3]
    row = jnp.zeros((1, LANES), jnp.float32)
    for k in range(count):
        row = jnp.where(lane == k, cell[0, 0, k].astype(jnp.float32), row)
        for t in range(steps):
            row = jnp.where(lane == count + k * steps + t, time_step * amp[0, 0, k, t], row)
    out[size - 1 : size, :] = row
    per_step = time_step * inner_coef
    lines = [jnp.zeros((1, LANES), jnp.float32) for _ in range(table.shape[0])]
    for k in range(kinds.shape[1]):
        decay = kinds[3, k]
        values = (
            kinds[0, k] * per_step,
            kinds[1, k] * per_step,
            kinds[2, k] * per_step,
            decay,
            (1.0 - decay) * kinds[4, k] * (half_step / time_step),
            kinds[5, k],
        )
        for i, value in enumerate(values):
            lines[i] = jnp.where(lane == k + 1, value, lines[i])
    for i, line in enumerate(lines):
        table[i : i + 1, :] = line
    for copy in copies:
        copy.wait()


def divisor(n, top):
    return max(k for k in range(1, top + 1) if n % k == 0)


class Layout:
    def __init__(self, cx, cy, steps, sources, window, dests, fixed):
        self.cx, self.cy, self.steps, self.sources = cx, cy, steps, sources
        self.window, self.dests, self.fixed = window, tuple(dests), fixed
        self.field = cx * cy
        self.margin = 4
        low = self.margin + cy - 3 * steps + 1
        self.rows = round_up(low + round_up(cy + 6 * steps - 2, SUB) + 2, SUB)

    def base_plane(self, s, me):
        if self.fixed is None:
            return jnp.bitwise_xor(me, self.dests[s]) * self.cx
        return self.fixed - self.dests[s] * self.cx

    def tiles(self, reach):
        return self.margin + self.cy - reach, -(-(self.cy + 2 * reach) // SUB)

    def planes(self, reach, me):
        if self.fixed is not None:
            return self.fixed - reach, self.cx + 2 * reach
        own = [w * self.cx for w in range(self.window // self.cx)]
        need = max(
            min(w + self.cx + reach, self.window) - max(w - reach, 0) for w in own
        )
        need += need % 2 if need < self.window else 0
        return jnp.clip(me * self.cx - reach, 0, self.window - need), need


class State:
    def __init__(self, vel, stress, mem):
        self.vel, self.stress, self.mem = vel, stress, mem


def unpack(lay, block, part, table, state, props, push_in, plane, row, last_step):
    cx, cy, sources, steps = lay.cx, lay.cy, lay.sources, lay.steps
    shape = (cy, LANES)
    size = block.shape[0]

    held = HELD[part]

    def piece(f, p):
        return block[pl.ds((f - held.start) * lay.field + p, cy, stride=cx), :]

    def copy_fields(p):
        for c in range(3):
            if VEL + c in held:
                state.vel[c, plane + p + 2, pl.ds(row, cy), :] = piece(VEL + c, p)
        for c in range(6):
            if STR + c in held:
                state.stress[c, plane + p + 2, pl.ds(row, cy), :] = piece(STR + c, p)
            if MEM + c in held:
                state.mem[c, plane + p, pl.ds(row, cy), :] = piece(MEM + c, p) * half_step

    if COD not in held:
        for p in range(cx):
            copy_fields(p)
        return

    line = block[size - 1 : size, :]
    spot = [
        jnp.broadcast_to(line[:, k : k + 1], shape) for k in range(sources * (1 + steps))
    ]
    number = lax.broadcasted_iota(jnp.int32, shape, 0) * LANES
    number = (number + lax.broadcasted_iota(jnp.int32, shape, 1)).astype(jnp.float32)
    lines = [jnp.broadcast_to(table[k : k + 1, :], (SUB, LANES)) for k in range(6)]
    across = cy // BLK
    for i in range(cx // BLK):
        first = len(held) * lay.field + i * across
        grow = jnp.concatenate(
            [
                jnp.broadcast_to(block[first + j : first + j + 1, :], (BLK, LANES))
                for j in range(across)
            ],
            axis=0,
        )
        for p in range(i * BLK, (i + 1) * BLK):
            copy_fields(p)
            code = jnp.clip(piece(COD, p).astype(jnp.int32), 0, LANES - 1)
            for lo in range(0, cy, SUB):
                n = min(SUB, cy - lo)
                index = code[lo : lo + n]
                for k in range(6):
                    value = jnp.take_along_axis(lines[k][:n], index, axis=1)
                    if k in (1, 2):
                        value = value * grow[lo : lo + n]
                    props[k, plane + p, pl.ds(row + lo, n), :] = value
            hits = [spot[k] == number + float(p * cy * LANES) for k in range(sources)]
            for t in range(last_step):
                total = jnp.zeros(shape, jnp.float32)
                for k in range(sources):
                    total = total + jnp.where(hits[k], spot[sources + k * steps + t], 0.0)
                push_in[t, plane + p, pl.ds(row, cy), :] = total


def deep(f, k):
    lane = lax.broadcasted_iota(jnp.int32, f.shape, 1)
    moved = pltpu.roll(f, (-k) % LANES, 1)
    keep = lane < LANES - k if k > 0 else lane >= -k
    return jnp.where(keep, moved, 0.0)


def z_back(f):
    return f - deep(f, -1), deep(f, 1) - deep(f, -2)


def z_fore(f):
    return deep(f, 1) - f, deep(f, 2) - deep(f, -1)


def add(*pairs):
    one, two = pairs[0]
    for a, b in pairs[1:]:
        one = one + a
        two = two + b
    return one - ratio * two


class Reader:
    def __init__(self, ref, c, p, r):
        self.ref, self.c, self.p, self.r = ref, c, p, r

    def at(self, dp=0, dr=0):
        return self.ref[self.c, self.p + 2 + dp, pl.ds(self.r + dr, SUB), :]

    def x_fore(self):
        return self.at(1) - self.at(0), self.at(2) - self.at(-1)

    def x_back(self):
        return self.at(0) - self.at(-1), self.at(1) - self.at(-2)

    def y_fore(self):
        return self.at(0, 1) - self.at(0, 0), self.at(0, 2) - self.at(0, -1)

    def y_back(self):
        return self.at(0, 0) - self.at(0, -1), self.at(0, 1) - self.at(0, -2)


def velocity_phase(old, new, props, first, n, start, count):
    def body(i, carry):
        p = first + i
        for r in [start + SUB * j for j in range(count)]:
            sxx, sxz, sxy, syz, syy, szz = [Reader(old.stress, c, p, r) for c in range(6)]
            push = props[0, p, pl.ds(r, SUB), :]
            forces = (
                add(sxx.x_fore(), sxy.y_back(), z_back(sxz.at())),
                add(sxy.x_back(), syy.y_fore(), z_back(syz.at())),
                add(sxz.x_back(), syz.y_back(), z_fore(szz.at())),
            )
            for c in range(3):
                now = old.vel[c, p + 2, pl.ds(r, SUB), :]
                new.vel[c, p + 2, pl.ds(r, SUB), :] = now + push * forces[c]
        return carry

    lax.fori_loop(0, n, body, 0, unroll=divisor(n, UNROLL[0]))


def stress_phase(lay, old, new, props, push_in, t, first, n, start, count, outs=None):
    def body(i, carry):
        p = first + i
        for j in range(count):
            r = start + SUB * j
            here = pl.ds(r, SUB)
            ve, vn, vd = [Reader(new.vel, c, p, r) for c in range(3)]
            exx = add(ve.x_back())
            eyy = add(vn.y_back())
            ezz = add(z_back(vd.at()))
            exz = add(z_fore(ve.at()), vd.x_fore())
            exy = add(ve.y_fore(), vn.x_fore())
            eyz = add(z_fore(vn.at()), vd.y_fore())
            mu = props[2, p, here, :]
            twice = mu + mu
            bulk = props[1, p, here, :] * (exx + eyy + ezz)
            moves = (
                bulk + twice * exx,
                mu * exz,
                mu * exy,
                mu * eyz,
                bulk + twice * eyy,
                bulk + twice * ezz,
            )
            keep = props[3, p, here, :]
            gain = props[4, p, here, :]
            source = push_in[t, p, here, :]
            trial = []
            rest = []
            for c in range(6):
                before = old.mem[c, p, here, :]
                after = keep * before + gain * moves[c]
                rest.append(after)
                now = old.stress[c, p + 2, here, :]
                if c in NORMAL:
                    now = now + source
                trial.append((now + moves[c]) - (before + after))
            mean = (trial[0] + trial[4] + trial[5]) * (1.0 / 3.0)
            dxx, dyy, dzz = trial[0] - mean, trial[4] - mean, trial[5] - mean
            dxz, dxy, dyz = trial[1], trial[2], trial[3]
            second = 0.5 * (dxx * dxx + dyy * dyy + dzz * dzz) + (
                dxz * dxz + dxy * dxy + dyz * dyz
            )
            soft = jnp.maximum(-mean, 0.0) + jnp.log(1.0 + jnp.exp(-jnp.abs(mean)))
            level = props[5, p, here, :] + friction * soft
            scaled = second / (level * level)
            grown = jnp.minimum(1.0 + scaled * scaled, largest)
            factor = lax.rsqrt(grown * lax.rsqrt(grown))
            done = (
                mean + factor * dxx,
                factor * dxz,
                factor * dxy,
                factor * dyz,
                mean + factor * dyy,
                mean + factor * dzz,
            )
            if outs is not None:
                lo = SUB * j
                n_rows = min(SUB, lay.cy - lo)

                def put(out, c, value):
                    at = c * lay.field + lo * lay.cx + i
                    out[pl.ds(at, n_rows, stride=lay.cx), :] = value[:n_rows]

                for c, part in enumerate((ve, vn, vd)):
                    put(outs[0], c, part.at())
                for c in range(6):
                    put(outs[1], c, done[c])
                    put(outs[2], c, rest[c] * (1.0 / half_step))
            else:
                for c in range(6):
                    new.stress[c, p + 2, here, :] = done[c]
                    new.mem[c, p, here, :] = rest[c]
        return carry

    lax.fori_loop(0, n, body, 0, unroll=divisor(n, UNROLL[1]))


CENTER, INNER, OUTER = 0, 1, 2
EARLY_STEPS = 2


def unpack_jobs(lay, blocks, jobs, table, state, props, push_in, me, odd):
    cy, margin, steps = lay.cy, lay.margin, lay.steps
    rows = (
        margin + cy,
        jnp.where(odd == 0, margin + 2 * cy, margin),
        jnp.where(odd == 0, margin, margin + 2 * cy),
    )
    for block, (s, kind, part) in zip(blocks, jobs):
        plane = lay.base_plane(s, me)
        pushes = steps if kind == CENTER else steps - 1
        unpack(lay, block, part, table, state, props, push_in, plane, rows[kind], pushes)


def states_of(refs):
    return [State(*refs[i : i + 3]) for i in range(0, len(refs), 3)]


def stage_kernel(*refs, lay, jobs, initial, final, held):
    blocks = refs[: len(jobs)]
    table, place = refs[len(jobs) : len(jobs) + 2]
    refs = refs[-held:]
    props, push_in = refs[:2]
    states = states_of(refs[2:])
    me, odd = place[0], lax.rem(place[1], 2)

    if initial:
        blank = jnp.zeros((lay.rows, LANES), jnp.float32)
        for p in (0, 1, lay.window + 2, lay.window + 3):
            for c in range(3):
                for i, state in enumerate(states):
                    if i > 0:
                        state.vel[c, p] = blank
                    state.stress[c, p] = blank
    unpack_jobs(lay, blocks, jobs, table, states[0], props, push_in, me, odd)
    if not final:
        return

    for t in range(len(states) - 1):
        for k in (0, 1):
            reach, late = split(lay, t, k)
            start, count = lay.tiles(reach)
            first, n = lay.planes(reach, me)
            end = start + lay.cy + 2 * reach
            at = jnp.where(odd == 0, end - SUB * (count - late), start)
            part = (first, n, at, count - late)
            if k == 0:
                velocity_phase(states[t], states[t + 1], props, *part)
            else:
                stress_phase(lay, states[t], states[t + 1], props, push_in, t, *part)


def split(lay, t, k):
    reach = 3 * (lay.steps - 1 - t) + (2 if k == 0 else 0)
    return reach, -(-(reach + 4 * t + 2 * k + 2) // SUB)


def late_kernel(*refs, lay, jobs, held):
    count = len(jobs)
    blocks = refs[:count]
    table, place = refs[count : count + 2]
    outs = refs[count + 2 + held : count + 5 + held]
    refs = refs[-held:]
    props, push_in = refs[:2]
    states = states_of(refs[2:])
    me, odd = place[0], lax.rem(place[1], 2)
    unpack_jobs(lay, blocks, jobs, table, states[0], props, push_in, me, odd)

    for t in range(lay.steps):
        for k in (0, 1):
            reach, late = split(lay, t, k)
            start, count = lay.tiles(reach)
            first, n = lay.planes(reach, me)
            if t + 1 < len(states):
                old, new = states[t], states[t + 1]
                end = start + lay.cy + 2 * reach
                part = (first, n, jnp.where(odd == 0, start, end - SUB * late), late)
            else:
                old = new = states[-1]
                part = (first, n, start, count)
            if k == 0:
                velocity_phase(old, new, props, *part)
            else:
                final = outs if t == lay.steps - 1 else None
                stress_phase(lay, old, new, props, push_in, t, *part, final)


def sees_all(n_we, width):
    return n_we <= 2 * width + 1 and n_we & (n_we - 1) == 0


def devices_in_view(n_we, width):
    return n_we if sees_all(n_we, width) else 2 * width + 1


def is_square(n_we, width):
    return sees_all(n_we, width) and n_we == 4


def shards(
    velocity, stress, memory, material_code, block_scale, material_table, source_cell, source_amp
):
    _, cx, cy, cz = velocity.shape
    sources, steps = source_amp.shape[2:]
    n_we, n_sn = lax.axis_size("we"), lax.axis_size("sn")
    reach = 3 * steps
    assert cz == LANES and cy >= reach and cx % BLK == 0 and cy % BLK == 0
    assert sources * (steps + 1) <= LANES

    used = FIELDS * cx * cy + (cx // BLK) * (cy // BLK) + 1
    vmem = pl.BlockSpec(memory_space=pltpu.VMEM)
    smem = pl.BlockSpec(memory_space=pltpu.SMEM)
    anywhere = pl.BlockSpec(memory_space=pl.ANY)

    def flat(x):
        return jnp.swapaxes(x, -3, -2).reshape(-1, LANES)

    assert material_table.shape[1] < LANES
    own, table = pl.pallas_call(
        functools.partial(pack_kernel, field=cx * cy),
        out_shape=[
            pltpu.VMEM((n, LANES), jnp.float32) for n in (round_up(used, SUB), SUB)
        ],
        in_specs=[anywhere, anywhere, anywhere, vmem, smem, smem, smem, smem],
        out_specs=[vmem, vmem],
        scratch_shapes=[pltpu.SemaphoreType.DMA((3,))],
        name="pack",
    )(
        flat(velocity),
        flat(stress),
        flat(memory),
        flat(material_code),
        jnp.swapaxes(block_scale, 0, 1),
        source_cell,
        source_amp,
        material_table,
    )

    width = -(-reach // cx)
    everything = sees_all(n_we, width)
    if everything:
        dests = list(range(n_we))
        window, fixed = n_we * cx, None
        moves = [[(i, i ^ k) for i in range(n_we)] for k in dests]
    else:
        dests = [0] + [sign * k for k in range(1, width + 1) for sign in (1, -1)]
        window, fixed = (2 * width + 1) * cx, width * cx
        moves = [[(i, i + k) for i in range(n_we) if 0 <= i + k < n_we] for k in dests]
    inner = [(i, i ^ 1) for i in range(n_sn) if i ^ 1 < n_sn]
    outer = [(i, i - 1 + 2 * (i % 2)) for i in range(n_sn)]
    outer = [(a, b) for a, b in outer if 0 <= b < n_sn]
    place = jnp.stack([lax.axis_index("we"), lax.axis_index("sn")])

    lay = Layout(cx, cy, steps, sources, window, dests, fixed)

    def frames(n, extra):
        return jax.ShapeDtypeStruct((n, window + extra, lay.rows, LANES), jnp.float32)

    early = min(EARLY_STEPS, steps - 1)
    state = [frames(6, 0), frames(steps, 0)]
    state += (early + 1) * [frames(3, 4), frames(6, 4), frames(6, 0)]
    params = pltpu.CompilerParams(vmem_limit_bytes=16 << 20)
    ready = {(0, CENTER, WHOLE): own}

    def send(block, axis, move, key):
        ready[key] = lax.ppermute(block, axis, move)

    last = len(dests) - 1
    assert last + 1 == devices_in_view(n_we, width)
    if is_square(n_we, width):
        half = SPLIT * cx * cy
        send(own, "we", moves[1], (1, CENTER, WHOLE))
        send(own, "we", moves[2], (2, CENTER, WHOLE))
        for i in range(3):
            block = ready[i, CENTER, WHOLE]
            send(block, "sn", outer, (i, OUTER, WHOLE))
            send(block, "sn", inner, (i, INNER, WHOLE))
        send(ready[1, CENTER, WHOLE][:half], "we", moves[2], (3, CENTER, FIRST))
        send(ready[2, CENTER, WHOLE][half:], "we", moves[1], (3, CENTER, SECOND))
        send(ready[3, CENTER, FIRST], "sn", outer, (3, OUTER, FIRST))
        send(ready[0, OUTER, WHOLE][half:], "we", moves[3], (3, OUTER, SECOND))
        send(ready[3, CENTER, FIRST], "sn", inner, (3, INNER, FIRST))
        send(ready[3, CENTER, SECOND], "sn", inner, (3, INNER, SECOND))
        plan = [
            [(0, CENTER, WHOLE)],
            [(k, CENTER, WHOLE) for k in (1, 2)] + [(0, INNER, WHOLE), (0, OUTER, WHOLE)],
            [(1, INNER, WHOLE), (1, OUTER, WHOLE)],
            [(3, CENTER, FIRST), (3, CENTER, SECOND), (2, INNER, WHOLE)]
            + [(3, INNER, FIRST), (3, INNER, SECOND)],
        ]
    else:
        plan = []
        for i, move in enumerate(moves):
            if i > 0:
                send(own, "we", move, (i, CENTER, WHOLE))
            block = ready[i, CENTER, WHOLE]
            send(block, "sn", outer, (i, OUTER, WHOLE))
            send(block, "sn", inner, (i, INNER, WHOLE))
            plan.append([(i, CENTER, WHOLE)])
            if i > 0:
                plan[i].append((i - 1, INNER, WHOLE))
            if i == last:
                plan[i].append((i, INNER, WHOLE))
            elif i > 0:
                plan[i].append((i - 1, OUTER, WHOLE))

    held = []
    for i, jobs in enumerate(plan):
        parts = [ready[job] for job in jobs]
        extra = len(parts) + 2
        held = pl.pallas_call(
            functools.partial(
                stage_kernel,
                lay=lay,
                jobs=jobs,
                initial=i == 0,
                final=i == len(plan) - 1,
                held=len(state),
            ),
            out_shape=state,
            in_specs=[vmem] * (extra - 1) + [smem] + [vmem] * len(held),
            out_specs=[vmem] * len(state),
            input_output_aliases={extra + k: k for k in range(len(held))},
            compiler_params=params,
        )(*parts, table, place, *held)
    done = [job for jobs in plan for job in jobs]
    jobs = [job for job in ready if job not in done]
    parts = [ready[job] for job in jobs]
    extra = len(parts) + 2
    results = [jax.ShapeDtypeStruct((n * cx * cy, LANES), jnp.float32) for n in (3, 6, 6)]
    outs = pl.pallas_call(
        functools.partial(late_kernel, lay=lay, jobs=jobs, held=len(state)),
        out_shape=results + state,
        in_specs=[vmem] * (extra - 1) + [smem] + [vmem] * len(state),
        out_specs=[vmem] * (3 + len(state)),
        input_output_aliases={extra + i: 3 + i for i in range(len(state))},
        compiler_params=params,
        name="late",
    )(*parts, table, place, *held)
    return tuple(jnp.swapaxes(x.reshape(-1, cy, cx, cz), 1, 2) for x in outs[:3])


def solution(mesh):
    in_specs = (
        P(None, "we", "sn", None),
        P(None, "we", "sn", None),
        P(None, "we", "sn", None),
        P("we", "sn", None),
        P("we", "sn", None),
        P(),
        P("we", "sn", None),
        P("we", "sn", None, None),
    )
    out_specs = (P(None, "we", "sn", None), P(None, "we", "sn", None), P(None, "we", "sn", None))

    def call(*args):
        step = jax.shard_map(
            shards, mesh=mesh, in_specs=in_specs, out_specs=out_specs, check_vma=False
        )
        return step(*args)

    return call
```

profile of v0, /device:TPU:1, one launch (start us, length us, event | category | flops | bytes accessed | tf_op | source)
XLA Modules:
  0.0 47.1 jit_solution(3993385261822941737)
XLA Ops:
  0.6 2.0 %pack.1 = (f32[776,128]{1,0:T(8,128)S(1)}, f32[8,128]{1,0:T(8,128)S(1)}) custom-call(f32[144,128]{1,0:T(8,128)} %bitcast.26, f32[288,128]{1,0:T(8,128)} %bitcast.24, f32[288,128]{1,0:T(8,128)} %bitcast.25, s32[48,128]{1,0:T(8,128)} %bitcast.27, f32[3,1,4]{2,1,0:T(1,128)} %bitcast.28, s32[1,1,4]{2,1,0:T(1,128)} %cell.1, f32[1,1,4,4]{3,2,1,0:T(4,128)} %amp.1, ...), custom_call_target="tpu_custom_call" | custom-call | tf_op jit(solution)/shard_map/pack/pallas_call | solution.py:442
  2.6 2.1 %collective-permute-start.2 = (f32[776,128]{1,0:T(8,128)S(1)}, f32[776,128]{1,0:T(8,128)S(1)}, u32[]{:S(2)}, u32[]{:S(2)}) collective-permute-start(f32[776,128]{1,0:T(8,128)S(1)} %get-tuple-element.52.refs_0_), channel_id=1, source_target_pairs={{0,8},{8,0},{16,24},{24,16},{1,9},{9,1},{17,25},{25,17},{2,10},{10... | collective-permute-start | bytes 1191944 | tf_op jit(solution)/shard_map/ppermute | solution.py:489
  4.7 1.2 %collective-permute-start = (f32[776,128]{1,0:T(8,128)S(1)}, f32[776,128]{1,0:T(8,128)S(1)}, u32[]{:S(2)}, u32[]{:S(2)}) collective-permute-start(f32[776,128]{1,0:T(8,128)S(1)} %get-tuple-element.52.refs_0_), channel_id=1, source_target_pairs={{0,16},{8,24},{16,0},{24,8},{1,17},{9,25},{17,1},{25,9},{2,18},{10... | collective-permute-start | bytes 1191944 | tf_op jit(solution)/shard_map/ppermute | solution.py:489
  5.9 4.3 %collective-permute-start.5 = (f32[776,128]{1,0:T(8,128)S(1)}, f32[776,128]{1,0:T(8,128)S(1)}, u32[]{:S(2)}, u32[]{:S(2)}) collective-permute-start(f32[776,128]{1,0:T(8,128)S(1)} %get-tuple-element.52.refs_0_), channel_id=1, source_target_pairs={{1,2},{2,1},{3,4},{4,3},{5,6},{6,5},{9,10},{10,9},{11,12},{12,11},... | collective-permute-start | bytes 1191944 | tf_op jit(solution)/shard_map/ppermute | solution.py:489
  10.3 0.1 collective-permute-start.13
  10.3 3.3 %collective-permute-done.2.refs_0_ = f32[776,128]{1,0:T(8,128)S(1)} collective-permute-done((f32[776,128]{1,0:T(8,128)S(1)}, f32[776,128]{1,0:T(8,128)S(1)}, u32[]{:S(2)}, u32[]{:S(2)}) %collective-permute-start.2) | collective-permute-done | bytes 397344 | tf_op jit(solution)/shard_map/ppermute | solution.py:489
  13.6 1.3 %collective-permute-start.11 = (f32[776,128]{1,0:T(8,128)S(1)}, f32[776,128]{1,0:T(8,128)S(1)}, u32[]{:S(2)}, u32[]{:S(2)}) collective-permute-start(f32[776,128]{1,0:T(8,128)S(1)} %collective-permute-done.2.refs_0_), channel_id=1, source_target_pairs={{0,1},{1,0},{2,3},{3,2},{4,5},{5,4},{6,7},{7,6},{8,9},{9,8},{10,11... | collective-permute-start | bytes 1191944 | tf_op jit(solution)/shard_map/ppermute | solution.py:489
  14.9 0.0 collective-permute-done.refs_1_
  14.9 1.5 %collective-permute-start.7 = (f32[392,128]{1,0:T(8,128)S(1)}, f32[392,128]{1,0:T(8,128)S(1)}, u32[]{:S(2)}, u32[]{:S(2)}) collective-permute-start(f32[392,128]{1,0:T(8,128)S(1)} %slice.14), channel_id=1, source_target_pairs={{0,8},{8,0},{16,24},{24,16},{1,9},{9,1},{17,25},{25,17},{2,10},{10... | collective-permute-start | bytes 602120 | tf_op jit(solution)/shard_map/ppermute | solution.py:489
  16.4 1.3 %collective-permute-start.3 = (f32[384,128]{1,0:T(8,128)S(1)}, f32[384,128]{1,0:T(8,128)}, u32[]{:S(2)}, u32[]{:S(2)}) collective-permute-start(f32[384,128]{1,0:T(8,128)S(1)} %slice.12), channel_id=1, source_target_pairs={{0,16},{8,24},{16,0},{24,8},{1,17},{9,25},{17,1},{25,9},{2,18},{10... | collective-permute-start | bytes 589832 | tf_op jit(solution)/shard_map/ppermute | solution.py:489
  17.7 0.0 collective-permute-done.5.refs_3_
  17.7 3.9 %collective-permute-start.12 = (f32[776,128]{1,0:T(8,128)S(1)}, f32[776,128]{1,0:T(8,128)S(1)}, u32[]{:S(2)}, u32[]{:S(2)}) collective-permute-start(f32[776,128]{1,0:T(8,128)S(1)} %collective-permute-done.2.refs_0_), channel_id=1, source_target_pairs={{1,2},{2,1},{3,4},{4,3},{5,6},{6,5},{9,10},{10,9},{11,12},{12,11},... | collective-permute-start | bytes 1191944 | tf_op jit(solution)/shard_map/ppermute | solution.py:489
  21.6 0.0 collective-permute-done.13.refs_2_
  21.6 0.1 collective-permute-start.8
  21.7 1.0 %collective-permute-done.3.refs_0_ = f32[384,128]{1,0:T(8,128)} collective-permute-done((f32[384,128]{1,0:T(8,128)S(1)}, f32[384,128]{1,0:T(8,128)}, u32[]{:S(2)}, u32[]{:S(2)}) %collective-permute-start.3) | collective-permute-done | bytes 196640 | tf_op jit(solution)/shard_map/ppermute | solution.py:489
  22.7 1.2 %collective-permute-start.9 = (f32[384,128]{1,0:T(8,128)}, f32[384,128]{1,0:T(8,128)S(1)}, u32[]{:S(2)}, u32[]{:S(2)}) collective-permute-start(f32[384,128]{1,0:T(8,128)} %collective-permute-done.3.refs_0_), channel_id=1, source_target_pairs={{0,1},{1,0},{2,3},{3,2},{4,5},{5,4},{6,7},{7,6},{8,9},{9,8},{10,11... | collective-permute-start | bytes 589832 | tf_op jit(solution)/shard_map/ppermute | solution.py:489
  23.9 0.0 collective-permute-done.7.refs_1_
  23.9 3.1 %collective-permute-start.1 = (f32[776,128]{1,0:T(8,128)S(1)}, f32[776,128]{1,0:T(8,128)S(1)}, u32[]{:S(2)}, u32[]{:S(2)}) collective-permute-start(f32[776,128]{1,0:T(8,128)S(1)} %collective-permute-done.refs_1_), channel_id=1, source_target_pairs={{1,2},{2,1},{3,4},{4,3},{5,6},{6,5},{9,10},{10,9},{11,12},{12,11},... | collective-permute-start | bytes 1191944 | tf_op jit(solution)/shard_map/ppermute | solution.py:489
  27.0 0.0 collective-permute-done.9.refs_3_
  27.0 0.0 copy-start.2
  27.0 0.7 %copy-done.2 = f32[384,128]{1,0:T(8,128)} copy-done((f32[384,128]{1,0:T(8,128)}, f32[384,128]{1,0:T(8,128)S(1)}, u32[]{:S(2)}) %copy-start.2) | copy-done | bytes 196632
  27.7 0.0 collective-permute-start.10
  27.7 0.7 %slice.13 = f32[392,128]{1,0:T(8,128)} slice(f32[776,128]{1,0:T(8,128)S(1)} %collective-permute-done.5.refs_3_), slice={[384:776], [0:128]} | slice | bytes 401408 | tf_op jit(solution)/shard_map/slice | solution.py:504
  28.4 0.0 collective-permute-done.11.refs_0_
  28.4 1.2 %collective-permute-start.6 = (f32[392,128]{1,0:T(8,128)}, f32[392,128]{1,0:T(8,128)}, u32[]{:S(2)}, u32[]{:S(2)}) collective-permute-start(f32[392,128]{1,0:T(8,128)} %slice.13), channel_id=1, source_target_pairs={{0,24},{8,16},{16,8},{24,0},{1,25},{9,17},{17,9},{25,1},{2,26},{10... | collective-permute-start | bytes 602120 | tf_op jit(solution)/shard_map/ppermute | solution.py:489
  29.6 0.0 collective-permute-done.12.refs_1_
  29.6 0.0 copy-start
  29.6 0.8 %copy-done = f32[776,128]{1,0:T(8,128)} copy-done((f32[776,128]{1,0:T(8,128)}, f32[776,128]{1,0:T(8,128)S(1)}, u32[]{:S(2)}) %copy-start) | copy-done | bytes 397336
  30.4 3.9 %collective-permute-start.4 = (f32[384,128]{1,0:T(8,128)}, f32[384,128]{1,0:T(8,128)}, u32[]{:S(2)}, u32[]{:S(2)}) collective-permute-start(f32[384,128]{1,0:T(8,128)} %collective-permute-done.3.refs_0_), channel_id=1, source_target_pairs={{1,2},{2,1},{3,4},{4,3},{5,6},{6,5},{9,10},{10,9},{11,12},{12,11},... | collective-permute-start | bytes 589832 | tf_op jit(solution)/shard_map/ppermute | solution.py:489
  34.2 0.1 pad_add_fusion.refs_2_.refs_5_.refs_3_.refs_6_.refs_4_
  34.3 0.8 %shard_map.103 = (f32[6,16,48,128]{3,2,1,0:T(8,128)S(1)}, f32[4,16,48,128]{3,2,1,0:T(8,128)S(1)}, f32[3,20,48,128]{3,2,1,0:T(8,128)S(1)}, f32[6,20,48,128]{3,2,1...) custom-call(f32[776,128]{1,0:T(8,128)S(1)} %get-tuple-element.52.ref, ...), custom_call_target="tpu_custom_call" | custom-call | tf_op jit(solution)/shard_map/pallas_call | solution.py:534
  35.1 0.0 copy-start.1
  35.1 1.3 %shard_map.104 = (f32[6,16,48,128]{3,2,1,0:T(8,128)S(1)}, f32[4,16,48,128]{3,2,1,0:T(8,128)S(1)}, f32[3,20,48,128]{3,2,1,0:T(8,128)S(1)}, f32[6,20,48,128]{3,2,1...) custom-call(f32[776,128]{1,0:T(8,128)S(1)} %collective-permute-done., ...), custom_call_target="tpu_custom_call", output_to_operand_aliasing={{0}: (6, {}), {1}: (7, {}), {2}: (8, {}), {3}: (9, {}), {4}... | custom-call | tf_op jit(solution)/shard_map/pallas_call | solution.py:534
  36.4 0.0 copy-done.1
  36.4 0.0 copy-start.3
  36.4 0.9 %shard_map.105 = (f32[6,16,48,128]{3,2,1,0:T(8,128)S(1)}, f32[4,16,48,128]{3,2,1,0:T(8,128)S(1)}, f32[3,20,48,128]{3,2,1,0:T(8,128)S(1)}, f32[6,20,48,128]{3,2,1...) custom-call(f32[776,128]{1,0:T(8,128)S(1)} %collective-permute-done., ...), custom_call_target="tpu_custom_call", output_to_operand_aliasing={{0}: (4, {}), {1}: (5, {}), {2}: (6, {}), {3}: (7, {}), {4}... | custom-call | tf_op jit(solution)/shard_map/pallas_call | solution.py:534
  37.3 0.0 collective-permute-done.8.refs_2_
  37.3 0.0 collective-permute-done.10.refs_4_
  37.3 0.1 copy-done.3
  37.3 3.6 %shard_map.106 = (f32[6,16,48,128]{3,2,1,0:T(8,128)S(1)}, f32[4,16,48,128]{3,2,1,0:T(8,128)S(1)}, f32[3,20,48,128]{3,2,1,0:T(8,128)S(1)}, f32[6,20,48,128]{3,2,1...) custom-call(f32[384,128]{1,0:T(8,128)} %collective-permute-done.3.re, ...), custom_call_target="tpu_custom_call", output_to_operand_aliasing={{0}: (7, {}), {1}: (8, {}), {2}: (9, {}), {3}: (10, {}), {4... | custom-call | tf_op jit(solution)/shard_map/pallas_call | solution.py:534
  41.0 0.0 collective-permute-done.6.refs_2_
  41.0 0.0 collective-permute-done.4.refs_1_
  41.0 0.0 collective-permute-done.1.refs_0_
  41.0 6.1 %late.1 = (f32[144,128]{1,0:T(8,128)}, f32[288,128]{1,0:T(8,128)}, f32[288,128]{1,0:T(8,128)}, f32[6,16,48,128]{3,2,1,0:T(8,128)S(1)}, f32[4,16,48,128]{3,2,1,0:...) custom-call(f32[776,128]{1,0:T(8,128)S(1)} %collective-permute-done., ...), custom_call_target="tpu_custom_call", output_to_operand_aliasing={{3}: (5, {}), {4}: (6, {}), {5}: (7, {}), {6}: (8, {}), {7}... | custom-call | tf_op jit(solution)/shard_map/late/pallas_call | solution.py:554
  (2 shorter events, 0.0 us)
Async XLA Ops:
  2.6 11.0 %collective-permute-start.2 = (f32[776,128]{1,0:T(8,128)S(1)}, f32[776,128]{1,0:T(8,128)S(1)}, u32[]{:S(2)}, u32[]{:S(2)}) collective-permute-start(f32[776,128]{1,0:T(8,128)S(1)} %get-tuple-element.52.refs_0_), channel_id=1, source_target_pairs={{0,8},{8,0},{16,24},{24,16},{1,9},{9,1},{17,25},{25,17},{2,10},{10... | collective-permute-start | bytes 1191944 | tf_op jit(solution)/shard_map/ppermute | solution.py:489
  4.7 10.2 %collective-permute-start = (f32[776,128]{1,0:T(8,128)S(1)}, f32[776,128]{1,0:T(8,128)S(1)}, u32[]{:S(2)}, u32[]{:S(2)}) collective-permute-start(f32[776,128]{1,0:T(8,128)S(1)} %get-tuple-element.52.refs_0_), channel_id=1, source_target_pairs={{0,16},{8,24},{16,0},{24,8},{1,17},{9,25},{17,1},{25,9},{2,18},{10... | collective-permute-start | bytes 1191944 | tf_op jit(solution)/shard_map/ppermute | solution.py:489
  5.9 11.8 %collective-permute-start.5 = (f32[776,128]{1,0:T(8,128)S(1)}, f32[776,128]{1,0:T(8,128)S(1)}, u32[]{:S(2)}, u32[]{:S(2)}) collective-permute-start(f32[776,128]{1,0:T(8,128)S(1)} %get-tuple-element.52.refs_0_), channel_id=1, source_target_pairs={{1,2},{2,1},{3,4},{4,3},{5,6},{6,5},{9,10},{10,9},{11,12},{12,11},... | collective-permute-start | bytes 1191944 | tf_op jit(solution)/shard_map/ppermute | solution.py:489
  10.3 11.4 %collective-permute-start.13 = (f32[776,128]{1,0:T(8,128)S(1)}, f32[776,128]{1,0:T(8,128)S(1)}, u32[]{:S(2)}, u32[]{:S(2)}) collective-permute-start(f32[776,128]{1,0:T(8,128)S(1)} %get-tuple-element.52.refs_0_), channel_id=1, source_target_pairs={{0,1},{1,0},{2,3},{3,2},{4,5},{5,4},{6,7},{7,6},{8,9},{9,8},{10,11... | collective-permute-start | bytes 1191944 | tf_op jit(solution)/shard_map/ppermute | solution.py:489
  13.6 14.8 %collective-permute-start.11 = (f32[776,128]{1,0:T(8,128)S(1)}, f32[776,128]{1,0:T(8,128)S(1)}, u32[]{:S(2)}, u32[]{:S(2)}) collective-permute-start(f32[776,128]{1,0:T(8,128)S(1)} %collective-permute-done.2.refs_0_), channel_id=1, source_target_pairs={{0,1},{1,0},{2,3},{3,2},{4,5},{5,4},{6,7},{7,6},{8,9},{9,8},{10,11... | collective-permute-start | bytes 1191944 | tf_op jit(solution)/shard_map/ppermute | solution.py:489
  14.9 9.0 %collective-permute-start.7 = (f32[392,128]{1,0:T(8,128)S(1)}, f32[392,128]{1,0:T(8,128)S(1)}, u32[]{:S(2)}, u32[]{:S(2)}) collective-permute-start(f32[392,128]{1,0:T(8,128)S(1)} %slice.14), channel_id=1, source_target_pairs={{0,8},{8,0},{16,24},{24,16},{1,9},{9,1},{17,25},{25,17},{2,10},{10... | collective-permute-start | bytes 602120 | tf_op jit(solution)/shard_map/ppermute | solution.py:489
  16.4 6.3 %collective-permute-start.3 = (f32[384,128]{1,0:T(8,128)S(1)}, f32[384,128]{1,0:T(8,128)}, u32[]{:S(2)}, u32[]{:S(2)}) collective-permute-start(f32[384,128]{1,0:T(8,128)S(1)} %slice.12), channel_id=1, source_target_pairs={{0,16},{8,24},{16,0},{24,8},{1,17},{9,25},{17,1},{25,9},{2,18},{10... | collective-permute-start | bytes 589832 | tf_op jit(solution)/shard_map/ppermute | solution.py:489
  17.7 11.9 %collective-permute-start.12 = (f32[776,128]{1,0:T(8,128)S(1)}, f32[776,128]{1,0:T(8,128)S(1)}, u32[]{:S(2)}, u32[]{:S(2)}) collective-permute-start(f32[776,128]{1,0:T(8,128)S(1)} %collective-permute-done.2.refs_0_), channel_id=1, source_target_pairs={{1,2},{2,1},{3,4},{4,3},{5,6},{6,5},{9,10},{10,9},{11,12},{12,11},... | collective-permute-start | bytes 1191944 | tf_op jit(solution)/shard_map/ppermute | solution.py:489
  21.6 15.6 %collective-permute-start.8 = (f32[776,128]{1,0:T(8,128)S(1)}, f32[776,128]{1,0:T(8,128)S(1)}, u32[]{:S(2)}, u32[]{:S(2)}) collective-permute-start(f32[776,128]{1,0:T(8,128)S(1)} %collective-permute-done.refs_1_), channel_id=1, source_target_pairs={{0,1},{1,0},{2,3},{3,2},{4,5},{5,4},{6,7},{7,6},{8,9},{9,8},{10,11... | collective-permute-start | bytes 1191944 | tf_op jit(solution)/shard_map/ppermute | solution.py:489
  22.7 4.3 %collective-permute-start.9 = (f32[384,128]{1,0:T(8,128)}, f32[384,128]{1,0:T(8,128)S(1)}, u32[]{:S(2)}, u32[]{:S(2)}) collective-permute-start(f32[384,128]{1,0:T(8,128)} %collective-permute-done.3.refs_0_), channel_id=1, source_target_pairs={{0,1},{1,0},{2,3},{3,2},{4,5},{5,4},{6,7},{7,6},{8,9},{9,8},{10,11... | collective-permute-start | bytes 589832 | tf_op jit(solution)/shard_map/ppermute | solution.py:489
  23.9 17.1 %collective-permute-start.1 = (f32[776,128]{1,0:T(8,128)S(1)}, f32[776,128]{1,0:T(8,128)S(1)}, u32[]{:S(2)}, u32[]{:S(2)}) collective-permute-start(f32[776,128]{1,0:T(8,128)S(1)} %collective-permute-done.refs_1_), channel_id=1, source_target_pairs={{1,2},{2,1},{3,4},{4,3},{5,6},{6,5},{9,10},{10,9},{11,12},{12,11},... | collective-permute-start | bytes 1191944 | tf_op jit(solution)/shard_map/ppermute | solution.py:489
  27.0 0.7 %copy-start.2 = (f32[384,128]{1,0:T(8,128)}, f32[384,128]{1,0:T(8,128)S(1)}, u32[]{:S(2)}) copy-start(f32[384,128]{1,0:T(8,128)S(1)} %collective-permute-done.9.refs_3_) | copy-start | bytes 589828
  27.7 9.6 %collective-permute-start.10 = (f32[392,128]{1,0:T(8,128)S(1)}, f32[392,128]{1,0:T(8,128)}, u32[]{:S(2)}, u32[]{:S(2)}) collective-permute-start(f32[392,128]{1,0:T(8,128)S(1)} %collective-permute-done.7.refs_1_), channel_id=1, source_target_pairs={{0,1},{1,0},{2,3},{3,2},{4,5},{5,4},{6,7},{7,6},{8,9},{9,8},{10,11... | collective-permute-start | bytes 602120 | tf_op jit(solution)/shard_map/ppermute | solution.py:489
  28.4 12.6 %collective-permute-start.6 = (f32[392,128]{1,0:T(8,128)}, f32[392,128]{1,0:T(8,128)}, u32[]{:S(2)}, u32[]{:S(2)}) collective-permute-start(f32[392,128]{1,0:T(8,128)} %slice.13), channel_id=1, source_target_pairs={{0,24},{8,16},{16,8},{24,0},{1,25},{9,17},{17,9},{25,1},{2,26},{10... | collective-permute-start | bytes 602120 | tf_op jit(solution)/shard_map/ppermute | solution.py:489
  29.6 0.8 %copy-start = (f32[776,128]{1,0:T(8,128)}, f32[776,128]{1,0:T(8,128)S(1)}, u32[]{:S(2)}) copy-start(f32[776,128]{1,0:T(8,128)S(1)} %collective-permute-done.12.refs_1_) | copy-start | bytes 1191940
  30.4 10.6 %collective-permute-start.4 = (f32[384,128]{1,0:T(8,128)}, f32[384,128]{1,0:T(8,128)}, u32[]{:S(2)}, u32[]{:S(2)}) collective-permute-start(f32[384,128]{1,0:T(8,128)} %collective-permute-done.3.refs_0_), channel_id=1, source_target_pairs={{1,2},{2,1},{3,4},{4,3},{5,6},{6,5},{9,10},{10,9},{11,12},{12,11},... | collective-permute-start | bytes 589832 | tf_op jit(solution)/shard_map/ppermute | solution.py:489
  35.1 1.3 %copy-start.1 = (f32[776,128]{1,0:T(8,128)S(1)}, f32[776,128]{1,0:T(8,128)}, u32[]{:S(2)}) copy-start(f32[776,128]{1,0:T(8,128)} %copy-done) | copy-start | bytes 1191940
  36.4 0.9 %copy-start.3 = (f32[384,128]{1,0:T(8,128)S(1)}, f32[384,128]{1,0:T(8,128)}, u32[]{:S(2)}) copy-start(f32[384,128]{1,0:T(8,128)} %copy-done.2) | copy-start | bytes 589828
where the time goes:
time: 47.4 us; the launch traced here: 47.1 us
  starting transfers between devices  25.1 us (53%)
  Pallas kernels  14.6 us (31%)
  waiting for transfers between devices  4.28 us (9%)
  local copies, waits for them, and re-layouts  2.21 us (5%)
  between operations  0.77 us (2%)
    ppermute x14, starting transfers between devices, send(): ready[key] = lax.ppermute(block, axis, move)  25.1 us
    pallas_call x4, Pallas kernels, shards(): pl.pallas_call(functools.partial(stage_kernel, lay=lay, jobs=jobs, initia...  6.55 us
    pallas_call x1, Pallas kernels, shards(): pl.pallas_call(functools.partial(late_kernel, lay=lay, jobs=jobs, held=le...  6.1 us
    ppermute x14, waiting for transfers between devices, send(): ready[key] = lax.ppermute(block, axis, move)  4.28 us
    pallas_call x1, Pallas kernels, shards(): pl.pallas_call(functools.partial(pack_kernel, field=cx * cy), out_shape=[...  1.97 us
    unnamed x8, local copies, waits for them, and re-layouts  1.5 us
  transfers between devices with their start and end apart: 14, of which 2 were waited for; matrix products, arithmetic and copies ran while one was open for 2% of the time, Pallas kernels for 14%

commit v1 on v0

--- a/solution.py
+++ b/solution.py
@@ -34,12 +34,25 @@
     return -(-value // step) * step
 
 
-def pack_kernel(vel, stress, mem, code, scale, cell, amp, kinds, out, table, sem, *, field):
+def pack_kernel(*refs, field):
+    vel, stress, mem = refs[:3]
+    out, table = refs[8:10]
+    near = refs[10:15]
+    sem = refs[15]
+    small = [
+        pltpu.make_async_copy(far, to, sem.at[3 + i])
+        for i, (far, to) in enumerate(zip(refs[3:8], near))
+    ]
+    for copy in small:
+        copy.start()
+    code, scale, cell, amp, kinds = near
     copies = []
     for i, (at, part) in enumerate(((VEL, vel), (STR, stress), (MEM, mem))):
         to = out.at[pl.ds(at * field, part.shape[0]), :]
         copies.append(pltpu.make_async_copy(part, to, sem.at[i]))
         copies[-1].start()
+    for copy in small:
+        copy.wait()
     out[COD * field : (COD + 1) * field, :] = (code[...] + 1).astype(jnp.float32)
     lane = lax.broadcasted_iota(jnp.int32, (1, LANES), 1)
     here = FIELDS * field
@@ -439,24 +452,24 @@
         return jnp.swapaxes(x, -3, -2).reshape(-1, LANES)
 
     assert material_table.shape[1] < LANES
+    small = (jnp.swapaxes(block_scale, 0, 1), source_cell, source_amp, material_table)
     own, table = pl.pallas_call(
         functools.partial(pack_kernel, field=cx * cy),
         out_shape=[
             pltpu.VMEM((n, LANES), jnp.float32) for n in (round_up(used, SUB), SUB)
         ],
-        in_specs=[anywhere, anywhere, anywhere, vmem, smem, smem, smem, smem],
+        in_specs=[anywhere] * 8,
         out_specs=[vmem, vmem],
-        scratch_shapes=[pltpu.SemaphoreType.DMA((3,))],
+        scratch_shapes=[pltpu.VMEM((cx * cy, LANES), jnp.int32)]
+        + [pltpu.SMEM(x.shape, x.dtype) for x in small]
+        + [pltpu.SemaphoreType.DMA((8,))],
         name="pack",
     )(
         flat(velocity),
         flat(stress),
         flat(memory),
         flat(material_code),
-        jnp.swapaxes(block_scale, 0, 1),
-        source_cell,
-        source_amp,
-        material_table,
+        *small,
     )
 
     width = -(-reach // cx)
@@ -509,7 +522,7 @@
             [(k, CENTER, WHOLE) for k in (1, 2)] + [(0, INNER, WHOLE), (0, OUTER, WHOLE)],
             [(1, INNER, WHOLE), (1, OUTER, WHOLE)],
             [(3, CENTER, FIRST), (3, CENTER, SECOND), (2, INNER, WHOLE)]
-            + [(3, INNER, FIRST), (3, INNER, SECOND)],
+            + [(3, INNER, FIRST), (3, INNER, SECOND), (2, OUTER, WHOLE)],
         ]
     else:
         plan = []

time: 47.4 us -> 45.3 us (0.956)
  starting transfers between devices: 25.1 us -> 23.3 us
  Pallas kernels: 14.6 us -> 13.7 us
  waiting for transfers between devices: 4.28 us -> 4.98 us
    ppermute x14, starting transfers between devices: 25.1 us -> 23.3 us  [send(): ready[key] = lax.ppermute(block, axis, move)]
    pallas_call x1, Pallas kernels: 1.97 us -> 1.11 us  [shards(): pl.pallas_call(functools.partial(pack_kernel, field=cx * cy), out_shape=[...]
    ppermute x14, waiting for transfers between devices: 4.28 us -> 4.98 us  [send(): ready[key] = lax.ppermute(block, axis, move)]
  transfers between devices with their start and end apart: 14 -> 14, of which waited for: 2 -> 2; matrix products, arithmetic and copies ran while one was open for 2% -> 2% of each run, Pallas kernels for 14% -> 15%
where the time goes in v1:
time: 45.3 us; the launch traced here: 45 us
  starting transfers between devices  23.3 us (51%)
  Pallas kernels  13.7 us (30%)
  waiting for transfers between devices  4.98 us (11%)
  local copies, waits for them, and re-layouts  2.21 us (5%)
  between operations  0.76 us (2%)
    ppermute x14, starting transfers between devices, send(): ready[key] = lax.ppermute(block, axis, move)  23.3 us
    pallas_call x4, Pallas kernels, shards(): pl.pallas_call(functools.partial(stage_kernel, lay=lay, jobs=jobs, initia...  6.78 us
    pallas_call x1, Pallas kernels, shards(): pl.pallas_call(functools.partial(late_kernel, lay=lay, jobs=jobs, held=le...  5.86 us
    ppermute x14, waiting for transfers between devices, send(): ready[key] = lax.ppermute(block, axis, move)  4.98 us
    unnamed x8, local copies, waits for them, and re-layouts  1.5 us
    pallas_call x1, Pallas kernels, shards(): pl.pallas_call(functools.partial(pack_kernel, field=cx * cy), out_shape=[...  1.11 us
  transfers between devices with their start and end apart: 14, of which 2 were waited for; matrix products, arithmetic and copies ran while one was open for 2% of the time, Pallas kernels for 15%

profile of v1, /device:TPU:1, one launch (start us, length us, event | category | flops | bytes accessed | tf_op | source)
XLA Modules:
  0.0 45.0 jit_solution(12003387020921107905)
XLA Ops:
  0.6 1.1 %pack.1 = (f32[776,128]{1,0:T(8,128)S(1)}, f32[8,128]{1,0:T(8,128)S(1)}) custom-call(f32[144,128]{1,0:T(8,128)} %bitcast.26, f32[288,128]{1,0:T(8,128)} %bitcast.24, f32[288,128]{1,0:T(8,128)} %bitcast.25, s32[48,128]{1,0:T(8,128)} %bitcast.27, f32[3,1,4]{2,1,0:T(1,128)} %bitcast.28, s32[1,1,4]{2,1,0:T(1,128)} %refs_5_.1, f32[1,1,4,4]{3,2,1,0:T(4,128)} %refs_6_.1, ...), custom_call_target="tpu_custom_call" | custom-call | tf_op jit(solution)/shard_map/pack/pallas_call | solution.py:456
  1.7 2.1 %collective-permute-start.5 = (f32[776,128]{1,0:T(8,128)S(1)}, f32[776,128]{1,0:T(8,128)S(1)}, u32[]{:S(2)}, u32[]{:S(2)}) collective-permute-start(f32[776,128]{1,0:T(8,128)S(1)} %get-tuple-element.52.refs_0_), channel_id=1, source_target_pairs={{0,16},{8,24},{16,0},{24,8},{1,17},{9,25},{17,1},{25,9},{2,18},{10... | collective-permute-start | bytes 1191944 | tf_op jit(solution)/shard_map/ppermute | solution.py:502
  3.9 1.2 %collective-permute-start = (f32[776,128]{1,0:T(8,128)S(1)}, f32[776,128]{1,0:T(8,128)S(1)}, u32[]{:S(2)}, u32[]{:S(2)}) collective-permute-start(f32[776,128]{1,0:T(8,128)S(1)} %get-tuple-element.52.refs_0_), channel_id=1, source_target_pairs={{0,8},{8,0},{16,24},{24,16},{1,9},{9,1},{17,25},{25,17},{2,10},{10... | collective-permute-start | bytes 1191944 | tf_op jit(solution)/shard_map/ppermute | solution.py:502
  5.1 4.3 %collective-permute-start.3 = (f32[776,128]{1,0:T(8,128)S(1)}, f32[776,128]{1,0:T(8,128)S(1)}, u32[]{:S(2)}, u32[]{:S(2)}) collective-permute-start(f32[776,128]{1,0:T(8,128)S(1)} %get-tuple-element.52.refs_0_), channel_id=1, source_target_pairs={{1,2},{2,1},{3,4},{4,3},{5,6},{6,5},{9,10},{10,9},{11,12},{12,11},... | collective-permute-start | bytes 1191944 | tf_op jit(solution)/shard_map/ppermute | solution.py:502
  9.4 0.1 collective-permute-start.13
  9.5 3.3 %collective-permute-done.5.refs_1_ = f32[776,128]{1,0:T(8,128)S(1)} collective-permute-done((f32[776,128]{1,0:T(8,128)S(1)}, f32[776,128]{1,0:T(8,128)S(1)}, u32[]{:S(2)}, u32[]{:S(2)}) %collective-permute-start.5) | collective-permute-done | bytes 397344 | tf_op jit(solution)/shard_map/ppermute | solution.py:502
  12.8 1.2 %collective-permute-start.6 = (f32[392,128]{1,0:T(8,128)S(1)}, f32[392,128]{1,0:T(8,128)}, u32[]{:S(2)}, u32[]{:S(2)}) collective-permute-start(f32[392,128]{1,0:T(8,128)S(1)} %slice.14), channel_id=1, source_target_pairs={{0,8},{8,0},{16,24},{24,16},{1,9},{9,1},{17,25},{25,17},{2,10},{10... | collective-permute-start | bytes 602120 | tf_op jit(solution)/shard_map/ppermute | solution.py:502
  14.0 0.0 collective-permute-done.refs_0_
  14.0 1.8 %collective-permute-start.11 = (f32[776,128]{1,0:T(8,128)S(1)}, f32[776,128]{1,0:T(8,128)S(1)}, u32[]{:S(2)}, u32[]{:S(2)}) collective-permute-start(f32[776,128]{1,0:T(8,128)S(1)} %collective-permute-done.refs_0_), channel_id=1, source_target_pairs={{0,1},{1,0},{2,3},{3,2},{4,5},{5,4},{6,7},{7,6},{8,9},{9,8},{10,11... | collective-permute-start | bytes 1191944 | tf_op jit(solution)/shard_map/ppermute | solution.py:502
  15.8 1.3 %collective-permute-start.1 = (f32[384,128]{1,0:T(8,128)S(1)}, f32[384,128]{1,0:T(8,128)}, u32[]{:S(2)}, u32[]{:S(2)}) collective-permute-start(f32[384,128]{1,0:T(8,128)S(1)} %slice.12), channel_id=1, source_target_pairs={{0,16},{8,24},{16,0},{24,8},{1,17},{9,25},{17,1},{25,9},{2,18},{10... | collective-permute-start | bytes 589832 | tf_op jit(solution)/shard_map/ppermute | solution.py:502
  17.1 0.0 collective-permute-done.3.refs_3_
  17.2 3.4 %collective-permute-start.12 = (f32[776,128]{1,0:T(8,128)S(1)}, f32[776,128]{1,0:T(8,128)S(1)}, u32[]{:S(2)}, u32[]{:S(2)}) collective-permute-start(f32[776,128]{1,0:T(8,128)S(1)} %collective-permute-done.refs_0_), channel_id=1, source_target_pairs={{1,2},{2,1},{3,4},{4,3},{5,6},{6,5},{9,10},{10,9},{11,12},{12,11},... | collective-permute-start | bytes 1191944 | tf_op jit(solution)/shard_map/ppermute | solution.py:502
  20.5 0.0 collective-permute-done.13.refs_2_
  20.5 2.2 %collective-permute-start.10 = (f32[776,128]{1,0:T(8,128)S(1)}, f32[776,128]{1,0:T(8,128)S(1)}, u32[]{:S(2)}, u32[]{:S(2)}) collective-permute-start(f32[776,128]{1,0:T(8,128)S(1)} %collective-permute-done.5.refs_1_), channel_id=1, source_target_pairs={{1,2},{2,1},{3,4},{4,3},{5,6},{6,5},{9,10},{10,9},{11,12},{12,11},... | collective-permute-start | bytes 1191944 | tf_op jit(solution)/shard_map/ppermute | solution.py:502
  22.7 0.0 collective-permute-done.1.refs_0_
  22.7 0.6 %collective-permute-start.7 = (f32[776,128]{1,0:T(8,128)S(1)}, f32[776,128]{1,0:T(8,128)S(1)}, u32[]{:S(2)}, u32[]{:S(2)}) collective-permute-start(f32[776,128]{1,0:T(8,128)S(1)} %collective-permute-done.5.refs_1_), channel_id=1, source_target_pairs={{0,1},{1,0},{2,3},{3,2},{4,5},{5,4},{6,7},{7,6},{8,9},{9,8},{10,11... | collective-permute-start | bytes 1191944 | tf_op jit(solution)/shard_map/ppermute | solution.py:502
  23.3 0.0 collective-permute-done.6.refs_1_
  23.3 0.0 collective-permute-start.8
  23.3 1.6 %collective-permute-done.8.refs_3_ = f32[384,128]{1,0:T(8,128)S(1)} collective-permute-done((f32[384,128]{1,0:T(8,128)}, f32[384,128]{1,0:T(8,128)S(1)}, u32[]{:S(2)}, u32[]{:S(2)}) %collective-permute-start.8) | collective-permute-done | bytes 196640 | tf_op jit(solution)/shard_map/ppermute | solution.py:502
  25.0 0.0 copy-start.2
  25.0 0.7 %copy-done.2 = f32[384,128]{1,0:T(8,128)} copy-done((f32[384,128]{1,0:T(8,128)}, f32[384,128]{1,0:T(8,128)S(1)}, u32[]{:S(2)}) %copy-start.2) | copy-done | bytes 196632
  25.7 0.4 collective-permute-start.9
  26.0 0.7 %slice.13 = f32[392,128]{1,0:T(8,128)} slice(f32[776,128]{1,0:T(8,128)S(1)} %collective-permute-done.3.refs_3_), slice={[384:776], [0:128]} | slice | bytes 401408 | tf_op jit(solution)/shard_map/slice | solution.py:517
  26.7 0.0 collective-permute-done.11.refs_0_
  26.7 1.2 %collective-permute-start.4 = (f32[392,128]{1,0:T(8,128)}, f32[392,128]{1,0:T(8,128)S(1)}, u32[]{:S(2)}, u32[]{:S(2)}) collective-permute-start(f32[392,128]{1,0:T(8,128)} %slice.13), channel_id=1, source_target_pairs={{0,24},{8,16},{16,8},{24,0},{1,25},{9,17},{17,9},{25,1},{2,26},{10... | collective-permute-start | bytes 602120 | tf_op jit(solution)/shard_map/ppermute | solution.py:502
  27.9 0.0 collective-permute-done.12.refs_1_
  27.9 0.0 copy-start
  27.9 0.8 %copy-done = f32[776,128]{1,0:T(8,128)} copy-done((f32[776,128]{1,0:T(8,128)}, f32[776,128]{1,0:T(8,128)S(1)}, u32[]{:S(2)}) %copy-start) | copy-done | bytes 397336
  28.7 3.5 %collective-permute-start.2 = (f32[384,128]{1,0:T(8,128)}, f32[384,128]{1,0:T(8,128)}, u32[]{:S(2)}, u32[]{:S(2)}) collective-permute-start(f32[384,128]{1,0:T(8,128)} %collective-permute-done.1.refs_0_), channel_id=1, source_target_pairs={{1,2},{2,1},{3,4},{4,3},{5,6},{6,5},{9,10},{10,9},{11,12},{12,11},... | collective-permute-start | bytes 589832 | tf_op jit(solution)/shard_map/ppermute | solution.py:502
  32.2 0.1 pad_add_fusion.refs_2_.refs_5_.refs_3_.refs_7_
  32.3 0.8 %shard_map.103 = (f32[6,16,48,128]{3,2,1,0:T(8,128)S(1)}, f32[4,16,48,128]{3,2,1,0:T(8,128)S(1)}, f32[3,20,48,128]{3,2,1,0:T(8,128)S(1)}, f32[6,20,48,128]{3,2,1...) custom-call(f32[776,128]{1,0:T(8,128)S(1)} %get-tuple-element.52.ref, ...), custom_call_target="tpu_custom_call" | custom-call | tf_op jit(solution)/shard_map/pallas_call | solution.py:547
  33.1 0.0 copy-start.1
  33.1 1.3 %shard_map.104 = (f32[6,16,48,128]{3,2,1,0:T(8,128)S(1)}, f32[4,16,48,128]{3,2,1,0:T(8,128)S(1)}, f32[3,20,48,128]{3,2,1,0:T(8,128)S(1)}, f32[6,20,48,128]{3,2,1...) custom-call(f32[776,128]{1,0:T(8,128)S(1)} %collective-permute-done., ...), custom_call_target="tpu_custom_call", output_to_operand_aliasing={{0}: (6, {}), {1}: (7, {}), {2}: (8, {}), {3}: (9, {}), {4}... | custom-call | tf_op jit(solution)/shard_map/pallas_call | solution.py:547
  34.4 0.0 copy-done.1
  34.4 0.0 copy-start.3
  34.4 0.9 %shard_map.105 = (f32[6,16,48,128]{3,2,1,0:T(8,128)S(1)}, f32[4,16,48,128]{3,2,1,0:T(8,128)S(1)}, f32[3,20,48,128]{3,2,1,0:T(8,128)S(1)}, f32[6,20,48,128]{3,2,1...) custom-call(f32[776,128]{1,0:T(8,128)S(1)} %collective-permute-done., ...), custom_call_target="tpu_custom_call", output_to_operand_aliasing={{0}: (4, {}), {1}: (5, {}), {2}: (6, {}), {3}: (7, {}), {4}... | custom-call | tf_op jit(solution)/shard_map/pallas_call | solution.py:547
  35.2 0.0 collective-permute-done.10.refs_5_
  35.2 0.0 collective-permute-done.7.refs_2_
  35.2 0.0 collective-permute-done.9.refs_4_
  35.2 0.1 copy-done.3
  35.3 3.9 %shard_map.106 = (f32[6,16,48,128]{3,2,1,0:T(8,128)S(1)}, f32[4,16,48,128]{3,2,1,0:T(8,128)S(1)}, f32[3,20,48,128]{3,2,1,0:T(8,128)S(1)}, f32[6,20,48,128]{3,2,1...) custom-call(f32[384,128]{1,0:T(8,128)} %collective-permute-done.1.re, ...), custom_call_target="tpu_custom_call", output_to_operand_aliasing={{0}: (8, {}), {1}: (9, {}), {2}: (10, {}), {3}: (11, {}), {... | custom-call | tf_op jit(solution)/shard_map/pallas_call | solution.py:547
  39.2 0.0 collective-permute-done.4.refs_1_
  39.2 0.0 collective-permute-done.2.refs_0_
  39.2 5.9 %late.1 = (f32[144,128]{1,0:T(8,128)}, f32[288,128]{1,0:T(8,128)}, f32[288,128]{1,0:T(8,128)}, f32[6,16,48,128]{3,2,1,0:T(8,128)S(1)}, f32[4,16,48,128]{3,2,1,0:...) custom-call(f32[384,128]{1,0:T(8,128)} %collective-permute-done.2.re, ...), custom_call_target="tpu_custom_call", output_to_operand_aliasing={{3}: (4, {}), {4}: (5, {}), {5}: (6, {}), {6}: (7, {}), {7}... | custom-call | tf_op jit(solution)/shard_map/late/pallas_call | solution.py:567
  (2 shorter events, 0.0 us)
Async XLA Ops:
  1.7 11.0 %collective-permute-start.5 = (f32[776,128]{1,0:T(8,128)S(1)}, f32[776,128]{1,0:T(8,128)S(1)}, u32[]{:S(2)}, u32[]{:S(2)}) collective-permute-start(f32[776,128]{1,0:T(8,128)S(1)} %get-tuple-element.52.refs_0_), channel_id=1, source_target_pairs={{0,16},{8,24},{16,0},{24,8},{1,17},{9,25},{17,1},{25,9},{2,18},{10... | collective-permute-start | bytes 1191944 | tf_op jit(solution)/shard_map/ppermute | solution.py:502
  3.9 10.1 %collective-permute-start = (f32[776,128]{1,0:T(8,128)S(1)}, f32[776,128]{1,0:T(8,128)S(1)}, u32[]{:S(2)}, u32[]{:S(2)}) collective-permute-start(f32[776,128]{1,0:T(8,128)S(1)} %get-tuple-element.52.refs_0_), channel_id=1, source_target_pairs={{0,8},{8,0},{16,24},{24,16},{1,9},{9,1},{17,25},{25,17},{2,10},{10... | collective-permute-start | bytes 1191944 | tf_op jit(solution)/shard_map/ppermute | solution.py:502
  5.1 12.1 %collective-permute-start.3 = (f32[776,128]{1,0:T(8,128)S(1)}, f32[776,128]{1,0:T(8,128)S(1)}, u32[]{:S(2)}, u32[]{:S(2)}) collective-permute-start(f32[776,128]{1,0:T(8,128)S(1)} %get-tuple-element.52.refs_0_), channel_id=1, source_target_pairs={{1,2},{2,1},{3,4},{4,3},{5,6},{6,5},{9,10},{10,9},{11,12},{12,11},... | collective-permute-start | bytes 1191944 | tf_op jit(solution)/shard_map/ppermute | solution.py:502
  9.4 11.1 %collective-permute-start.13 = (f32[776,128]{1,0:T(8,128)S(1)}, f32[776,128]{1,0:T(8,128)S(1)}, u32[]{:S(2)}, u32[]{:S(2)}) collective-permute-start(f32[776,128]{1,0:T(8,128)S(1)} %get-tuple-element.52.refs_0_), channel_id=1, source_target_pairs={{0,1},{1,0},{2,3},{3,2},{4,5},{5,4},{6,7},{7,6},{8,9},{9,8},{10,11... | collective-permute-start | bytes 1191944 | tf_op jit(solution)/shard_map/ppermute | solution.py:502
  12.8 10.5 %collective-permute-start.6 = (f32[392,128]{1,0:T(8,128)S(1)}, f32[392,128]{1,0:T(8,128)}, u32[]{:S(2)}, u32[]{:S(2)}) collective-permute-start(f32[392,128]{1,0:T(8,128)S(1)} %slice.14), channel_id=1, source_target_pairs={{0,8},{8,0},{16,24},{24,16},{1,9},{9,1},{17,25},{25,17},{2,10},{10... | collective-permute-start | bytes 602120 | tf_op jit(solution)/shard_map/ppermute | solution.py:502
  14.0 12.7 %collective-permute-start.11 = (f32[776,128]{1,0:T(8,128)S(1)}, f32[776,128]{1,0:T(8,128)S(1)}, u32[]{:S(2)}, u32[]{:S(2)}) collective-permute-start(f32[776,128]{1,0:T(8,128)S(1)} %collective-permute-done.refs_0_), channel_id=1, source_target_pairs={{0,1},{1,0},{2,3},{3,2},{4,5},{5,4},{6,7},{7,6},{8,9},{9,8},{10,11... | collective-permute-start | bytes 1191944 | tf_op jit(solution)/shard_map/ppermute | solution.py:502
  15.8 6.9 %collective-permute-start.1 = (f32[384,128]{1,0:T(8,128)S(1)}, f32[384,128]{1,0:T(8,128)}, u32[]{:S(2)}, u32[]{:S(2)}) collective-permute-start(f32[384,128]{1,0:T(8,128)S(1)} %slice.12), channel_id=1, source_target_pairs={{0,16},{8,24},{16,0},{24,8},{1,17},{9,25},{17,1},{25,9},{2,18},{10... | collective-permute-start | bytes 589832 | tf_op jit(solution)/shard_map/ppermute | solution.py:502
  17.2 10.8 %collective-permute-start.12 = (f32[776,128]{1,0:T(8,128)S(1)}, f32[776,128]{1,0:T(8,128)S(1)}, u32[]{:S(2)}, u32[]{:S(2)}) collective-permute-start(f32[776,128]{1,0:T(8,128)S(1)} %collective-permute-done.refs_0_), channel_id=1, source_target_pairs={{1,2},{2,1},{3,4},{4,3},{5,6},{6,5},{9,10},{10,9},{11,12},{12,11},... | collective-permute-start | bytes 1191944 | tf_op jit(solution)/shard_map/ppermute | solution.py:502
  20.5 14.7 %collective-permute-start.10 = (f32[776,128]{1,0:T(8,128)S(1)}, f32[776,128]{1,0:T(8,128)S(1)}, u32[]{:S(2)}, u32[]{:S(2)}) collective-permute-start(f32[776,128]{1,0:T(8,128)S(1)} %collective-permute-done.5.refs_1_), channel_id=1, source_target_pairs={{1,2},{2,1},{3,4},{4,3},{5,6},{6,5},{9,10},{10,9},{11,12},{12,11},... | collective-permute-start | bytes 1191944 | tf_op jit(solution)/shard_map/ppermute | solution.py:502
  22.7 12.5 %collective-permute-start.7 = (f32[776,128]{1,0:T(8,128)S(1)}, f32[776,128]{1,0:T(8,128)S(1)}, u32[]{:S(2)}, u32[]{:S(2)}) collective-permute-start(f32[776,128]{1,0:T(8,128)S(1)} %collective-permute-done.5.refs_1_), channel_id=1, source_target_pairs={{0,1},{1,0},{2,3},{3,2},{4,5},{5,4},{6,7},{7,6},{8,9},{9,8},{10,11... | collective-permute-start | bytes 1191944 | tf_op jit(solution)/shard_map/ppermute | solution.py:502
  23.3 1.7 %collective-permute-start.8 = (f32[384,128]{1,0:T(8,128)}, f32[384,128]{1,0:T(8,128)S(1)}, u32[]{:S(2)}, u32[]{:S(2)}) collective-permute-start(f32[384,128]{1,0:T(8,128)} %collective-permute-done.1.refs_0_), channel_id=1, source_target_pairs={{0,1},{1,0},{2,3},{3,2},{4,5},{5,4},{6,7},{7,6},{8,9},{9,8},{10,11... | collective-permute-start | bytes 589832 | tf_op jit(solution)/shard_map/ppermute | solution.py:502
  25.0 0.7 %copy-start.2 = (f32[384,128]{1,0:T(8,128)}, f32[384,128]{1,0:T(8,128)S(1)}, u32[]{:S(2)}) copy-start(f32[384,128]{1,0:T(8,128)S(1)} %collective-permute-done.8.refs_3_) | copy-start | bytes 589828
  25.7 9.6 %collective-permute-start.9 = (f32[392,128]{1,0:T(8,128)}, f32[392,128]{1,0:T(8,128)}, u32[]{:S(2)}, u32[]{:S(2)}) collective-permute-start(f32[392,128]{1,0:T(8,128)} %collective-permute-done.6.refs_1_), channel_id=1, source_target_pairs={{0,1},{1,0},{2,3},{3,2},{4,5},{5,4},{6,7},{7,6},{8,9},{9,8},{10,11... | collective-permute-start | bytes 602120 | tf_op jit(solution)/shard_map/ppermute | solution.py:502
  26.7 12.4 %collective-permute-start.4 = (f32[392,128]{1,0:T(8,128)}, f32[392,128]{1,0:T(8,128)S(1)}, u32[]{:S(2)}, u32[]{:S(2)}) collective-permute-start(f32[392,128]{1,0:T(8,128)} %slice.13), channel_id=1, source_target_pairs={{0,24},{8,16},{16,8},{24,0},{1,25},{9,17},{17,9},{25,1},{2,26},{10... | collective-permute-start | bytes 602120 | tf_op jit(solution)/shard_map/ppermute | solution.py:502
  27.9 0.8 %copy-start = (f32[776,128]{1,0:T(8,128)}, f32[776,128]{1,0:T(8,128)S(1)}, u32[]{:S(2)}) copy-start(f32[776,128]{1,0:T(8,128)S(1)} %collective-permute-done.12.refs_1_) | copy-start | bytes 1191940
  28.7 10.5 %collective-permute-start.2 = (f32[384,128]{1,0:T(8,128)}, f32[384,128]{1,0:T(8,128)}, u32[]{:S(2)}, u32[]{:S(2)}) collective-permute-start(f32[384,128]{1,0:T(8,128)} %collective-permute-done.1.refs_0_), channel_id=1, source_target_pairs={{1,2},{2,1},{3,4},{4,3},{5,6},{6,5},{9,10},{10,9},{11,12},{12,11},... | collective-permute-start | bytes 589832 | tf_op jit(solution)/shard_map/ppermute | solution.py:502
  33.1 1.3 %copy-start.1 = (f32[776,128]{1,0:T(8,128)S(1)}, f32[776,128]{1,0:T(8,128)}, u32[]{:S(2)}) copy-start(f32[776,128]{1,0:T(8,128)} %copy-done) | copy-start | bytes 1191940
  34.4 0.9 %copy-start.3 = (f32[384,128]{1,0:T(8,128)S(1)}, f32[384,128]{1,0:T(8,128)}, u32[]{:S(2)}) copy-start(f32[384,128]{1,0:T(8,128)} %copy-done.2) | copy-start | bytes 589828
